TPU v7x, 128 devices: a whole 4x4x4 slice. The times are simulated.
128 devices in a mesh: freq: 4 (over x), tile: 32 (over z, y, core).
Axes of the slice: x: 4, y: 4, z: 4, core: 2. Of those that a mesh axis runs over, the one named last changes fastest.
Arguments:
- u_data: bfloat16 [8, 16384, 128], P('freq', 'tile'), may hold values from -6 to 6
- u_basis: bfloat16 [8, 64, 64, 2, 48, 256], P('freq', 'tile'), may hold values from -0.25 to 0.25
- v_basis: bfloat16 [8, 64, 64, 2, 48, 256], P('freq', None, 'tile'), may hold values from -0.109375 to 0.109375
- ranks: int32 [8, 64, 64], P('freq'), may hold values from 8 to 48, as said below
- time_mask: int32 [64, 64], replicated, may hold values 0 or 1
Outputs:
- result: bfloat16 [8, 16384, 128], P('freq', 'tile')
Inputs may be any that keep to these rules, and one draw needn't show every extreme that they name: For every tile and every m, ranks[2 m + 1, i, j] = 56 - ranks[2 m, i, j].
All inputs are finite; a program needn't handle non-finite values.
Results may differ from a plain program's by a relative error of at most 0.006.
Values may be sent and summed in bfloat16 or wider, within the bound.
A program may use at most 128 MiB of HBM per device.

v0:
```python
import math

import jax
import jax.numpy as jnp
import numpy as np
from jax import lax
from jax.experimental import pallas as pl
from jax.experimental.pallas import tpu as pltpu
from jax.sharding import PartitionSpec as P

MESH = pl.DeviceIdType.MESH
PEERS = 32
GROUP = 4
GROUPS = PEERS // GROUP
SLOTS = 48
PAIR = 56
WIDTH = 128
TILE = 256
LAGS = 15


def lag_table(times):
    table = np.zeros((times, 128), np.float32)
    t = np.arange(times)
    for lag in range(-7, 8):
        angle = 2.0 * math.pi * ((lag * t) % times) / times
        table[:, 2 * (lag + 7)] = np.cos(angle) / times
        table[:, 2 * (lag + 7) + 1] = np.sin(angle) / times
    return table


def place(slot, sign):
    me = lax.axis_index("tile")
    offset = (13 * slot) % PEERS
    z = (me // 8 + sign * (offset // 8) + 4) % 4
    y = ((me // 2) % 4 + sign * ((offset // 2) % 4) + 4) % 4
    c = (me % 2 + offset % 2) % 2
    return z * 8 + y * 2 + c


def flip8(x):
    rows = lax.broadcasted_iota(jnp.int32, (8, WIDTH), 0)
    return jnp.take_along_axis(x, 7 - rows, axis=0)


def pack(first, second, rank):
    rows = lax.broadcasted_iota(jnp.int32, (8, WIDTH), 0)
    parts = [first[0:8]]
    for v in range(1, 6):
        other = flip8(second[8 * (6 - v) : 8 * (6 - v) + 8])
        parts.append(jnp.where(rows + 8 * v < rank, first[8 * v : 8 * v + 8], other))
    parts.append(flip8(second[0:8]))
    return parts


def unpack(packed, rank):
    rows = lax.broadcasted_iota(jnp.int32, (8, WIDTH), 0)
    first, second = [], []
    for v in range(6):
        first.append(jnp.where(rows + 8 * v < rank, packed[v], 0.0))
        second.append(jnp.where(rows + 8 * v < PAIR - rank, flip8(packed[6 - v]), 0.0))
    return jnp.concatenate(first, axis=0), jnp.concatenate(second, axis=0)


def turned(x):
    lanes = lax.broadcasted_iota(jnp.int32, x.shape, 1)
    rolled = pltpu.roll(x, WIDTH // 2, 1)
    return jnp.where(lanes < WIDTH // 2, -rolled, rolled)


def kernel(
    u_hbm, ub_hbm, vb_hbm, ranks_hbm, mask_hbm, table_hbm, out_ref,
    u_buf, ub, vb, ranks, mask, table, weights, lags,
    send, recv, z_send, z_recv, z_acc, r_acc,
    in_sem, u_sem, v_sem, send_sem, recv_sem, zs_sem, zr_sem,
):
    me = lax.axis_index("tile")
    fx = lax.axis_index("freq")
    barrier = pltpu.get_barrier_semaphore()

    def greet(slot, carry):
        pl.semaphore_signal(barrier, inc=1, device_id={"tile": place(slot, 1)}, device_id_type=MESH)
        return carry

    lax.fori_loop(1, PEERS, greet, 0)
    for dx in (1, 2, 3):
        pl.semaphore_signal(barrier, inc=1, device_id={"freq": (fx + dx) % 4}, device_id_type=MESH)

    copies = [
        pltpu.make_async_copy(u_hbm, u_buf, in_sem.at[0]),
        pltpu.make_async_copy(ranks_hbm, ranks, in_sem.at[1]),
        pltpu.make_async_copy(mask_hbm, mask, in_sem.at[2]),
        pltpu.make_async_copy(table_hbm, table, in_sem.at[3]),
    ]
    for copy in copies:
        copy.start()

    def u_copy(jj, slot):
        j = 2 * place(slot, 1) + jj
        return pltpu.make_async_copy(ub_hbm.at[:, :, j], ub.at[:, :, j], u_sem.at[jj, slot])

    def v_copy(jj, slot):
        i = 2 * place(slot, -1)
        return pltpu.make_async_copy(
            vb_hbm.at[:, pl.ds(i, 2), jj], vb.at[:, pl.ds(i, 2), jj], v_sem.at[jj, slot]
        )

    for jj in range(2):
        def fetch_u(slot, carry):
            u_copy(jj, slot).start()
            return carry
        lax.fori_loop(0, PEERS, fetch_u, 0)
    for jj in range(2):
        def fetch_v(slot, carry):
            v_copy(jj, slot).start()
            return carry
        lax.fori_loop(0, PEERS, fetch_v, 0)

    def remote(stage, jj, slot):
        return pltpu.make_async_remote_copy(
            src_ref=send.at[stage, jj, slot],
            dst_ref=recv.at[stage, jj, slot],
            send_sem=send_sem.at[stage, jj, slot],
            recv_sem=recv_sem.at[stage, jj, slot],
            device_id={"tile": place(slot, 1)},
            device_id_type=MESH,
        )

    def stay(stage, jj):
        return pltpu.make_async_copy(
            send.at[stage, jj, 0], recv.at[stage, jj, 0], recv_sem.at[stage, jj, 0]
        )

    def dispatch(stage, jj, group):
        @pl.when(group == 0)
        def _():
            stay(stage, jj).start()

        @pl.when(group > 0)
        def _():
            remote(stage, jj, GROUP * group).start()

        for k in range(1, GROUP):
            remote(stage, jj, GROUP * group + k).start()

    def arrive(stage, jj, group):
        @pl.when(group == 0)
        def _():
            stay(stage, jj).wait()

        @pl.when(group > 0)
        def _():
            remote(stage, jj, GROUP * group).wait_recv()

        for k in range(1, GROUP):
            remote(stage, jj, GROUP * group + k).wait_recv()

    copies[0].wait()
    for f in range(2):
        for i in range(2):
            x = u_buf[f, 256 * i : 256 * i + 256, :].astype(jnp.float32)
            weights[f, i, 0:256, :] = x.astype(jnp.bfloat16)
            weights[f, i, 256:512, :] = (-turned(x)).astype(jnp.bfloat16)
    copies[1].wait()

    def product(tiles, f, i):
        real = jnp.concatenate([t[0] for t in tiles], axis=0)
        imag = jnp.concatenate([t[1] for t in tiles], axis=0)
        lhs = jnp.concatenate([real, imag], axis=1)
        return jnp.dot(lhs, weights[f, i], preferred_element_type=jnp.float32)

    def emit(stage, jj, group, parts):
        for k in range(GROUP):
            block = jnp.concatenate(parts[0][k] + parts[1][k], axis=0)
            send[stage, jj, GROUP * group + k] = block.astype(jnp.bfloat16)

    def adjoint(jj, group, carry):
        where = [place(GROUP * group + k, 1) for k in range(GROUP)]
        for k in range(GROUP):
            u_copy(jj, GROUP * group + k).wait()
        parts = []
        for i in range(2):
            both = [product([ub[f, i, 2 * d + jj] for d in where], f, i) for f in range(2)]
            parts.append([
                pack(both[0][48 * k : 48 * k + 48], both[1][48 * k : 48 * k + 48],
                     ranks[0, 2 * me + i, 2 * where[k] + jj])
                for k in range(GROUP)
            ])

        @pl.when(group > 0)
        def _():
            dispatch(0, jj, group - 1)

        emit(0, jj, group, parts)
        return carry

    adjoint(0, 0, 0)
    pl.semaphore_wait(barrier, PEERS - 1 + 3)
    lax.fori_loop(1, GROUPS, lambda g, c: adjoint(0, g, c), 0)
    dispatch(0, 0, GROUPS - 1)
    lax.fori_loop(0, GROUPS, lambda g, c: adjoint(1, g, c), 0)
    dispatch(0, 1, GROUPS - 1)

    copies[2].wait()
    copies[3].wait()
    kept = mask[...].astype(jnp.float32)
    mixing = lax.dot_general(
        kept, table[...], (((0,), (0,)), ((), ())),
        precision=lax.Precision.HIGHEST, preferred_element_type=jnp.float32,
    )
    for lag in range(LAGS):
        for part in range(2):
            column = mixing[:, 2 * lag + part : 2 * lag + part + 1]
            lags[lag, part] = jnp.broadcast_to(column, (64, 128))

    def gather(jj, group, carry):
        whence = [place(GROUP * group + k, -1) for k in range(GROUP)]
        arrive(0, jj, group)
        stacks = [[], []]
        for k in range(GROUP):
            v_copy(jj, GROUP * group + k).wait()
            block = recv[0, jj, GROUP * group + k].astype(jnp.float32)
            for i in range(2):
                pieces = [block[56 * i + 8 * v : 56 * i + 8 * v + 8] for v in range(7)]
                pair = unpack(pieces, ranks[0, 2 * whence[k] + i, 2 * me + jj])
                for f in range(2):
                    stacks[f] += [pair[f], turned(pair[f])]
        for f in range(2):
            lhs = jnp.concatenate([s.astype(jnp.bfloat16) for s in stacks[f]], axis=0)
            rhs = jnp.concatenate(
                [vb[f, 2 * d + i, jj, c] for d in whence for i in range(2) for c in range(2)], axis=0
            )
            z_acc[f] += lax.dot_general(
                lhs, rhs, (((0,), (0,)), ((), ())), preferred_element_type=jnp.float32
            )
        return carry

    def clear():
        z_acc[...] = jnp.zeros_like(z_acc)

    def z_copy(jj, dx):
        return pltpu.make_async_remote_copy(
            src_ref=z_send.at[jj],
            dst_ref=z_recv.at[jj, dx - 1],
            send_sem=zs_sem.at[jj, dx - 1],
            recv_sem=zr_sem.at[jj, dx - 1],
            device_id={"freq": (fx + dx) % 4},
            device_id_type=MESH,
        )

    def share(jj):
        z_send[jj] = z_acc[...].astype(jnp.bfloat16)
        for dx in (2, 1, 3):
            z_copy(jj, dx).start()

    def mix(jj):
        for dx in (1, 3, 2):
            z_copy(jj, dx).wait_recv()
        for f in range(2):
            halves = []
            for h in range(2):
                cut = slice(128 * h, 128 * h + 128)
                real = jnp.zeros((64, 128), jnp.float32)
                imag = jnp.zeros((64, 128), jnp.float32)
                for dx in range(4):
                    for g in range(2):
                        held = z_send.at[jj] if dx == 0 else z_recv.at[jj, dx - 1]
                        zr = held[g, 0:64, cut].astype(jnp.float32)
                        zi = held[g, 64:128, cut].astype(jnp.float32)
                        lag = 2 * ((fx - dx + 4) % 4 - fx) + g - f + 7
                        cr = lags[lag, 0]
                        ci = lags[lag, 1]
                        real += cr * zr - ci * zi
                        imag += cr * zi + ci * zr
                halves.append((real, imag))
            for h in range(2):
                real, imag = halves[h]
                straight = jnp.concatenate([real, imag], axis=0)
                crossed = jnp.concatenate([imag, -real], axis=0)
                weights[f, 0, 128 * h : 128 * h + 128, :] = straight.T.astype(jnp.bfloat16)
                weights[f, 0, 256 + 128 * h : 384 + 128 * h, :] = crossed.T.astype(jnp.bfloat16)

    def forward(jj, group, carry):
        where = [place(GROUP * group + k, 1) for k in range(GROUP)]
        parts = []
        for i in range(2):
            both = [product([vb[f, 2 * d + i, jj] for d in where], f, 0) for f in range(2)]
            parts.append([
                pack(both[0][48 * k : 48 * k + 48], both[1][48 * k : 48 * k + 48],
                     ranks[0, 2 * where[k] + i, 2 * me + jj])
                for k in range(GROUP)
            ])

        @pl.when(group > 0)
        def _():
            dispatch(1, jj, group - 1)

        emit(1, jj, group, parts)
        return carry

    def finish(jj, group, carry):
        whence = [place(GROUP * group + k, -1) for k in range(GROUP)]
        arrive(1, jj, group)
        stacks = [[[], []], [[], []]]
        for k in range(GROUP):
            block = recv[1, jj, GROUP * group + k].astype(jnp.float32)
            for i in range(2):
                pieces = [block[56 * i + 8 * v : 56 * i + 8 * v + 8] for v in range(7)]
                pair = unpack(pieces, ranks[0, 2 * me + i, 2 * whence[k] + jj])
                for f in range(2):
                    stacks[f][i] += [pair[f], turned(pair[f])]
        for f in range(2):
            for i in range(2):
                lhs = jnp.concatenate([s.astype(jnp.bfloat16) for s in stacks[f][i]], axis=0)
                rhs = jnp.concatenate(
                    [ub[f, i, 2 * d + jj, c] for d in whence for c in range(2)], axis=0
                )
                r_acc[f, i] += lax.dot_general(
                    lhs, rhs, (((0,), (0,)), ((), ())), preferred_element_type=jnp.float32
                )
        return carry

    clear()
    r_acc[...] = jnp.zeros_like(r_acc)
    lax.fori_loop(0, GROUPS, lambda g, c: gather(0, g, c), 0)
    share(0)
    clear()
    ahead = 5
    lax.fori_loop(0, ahead, lambda g, c: gather(1, g, c), 0)
    mix(0)
    lax.fori_loop(0, GROUPS, lambda g, c: forward(0, g, c), 0)
    dispatch(1, 0, GROUPS - 1)
    lax.fori_loop(ahead, GROUPS, lambda g, c: gather(1, g, c), 0)
    share(1)
    lax.fori_loop(0, ahead, lambda g, c: finish(0, g, c), 0)
    mix(1)
    lax.fori_loop(0, GROUPS, lambda g, c: forward(1, g, c), 0)
    dispatch(1, 1, GROUPS - 1)
    lax.fori_loop(ahead, GROUPS, lambda g, c: finish(0, g, c), 0)
    lax.fori_loop(0, GROUPS, lambda g, c: finish(1, g, c), 0)
    for f in range(2):
        for i in range(2):
            out_ref[f, 256 * i : 256 * i + 256, :] = r_acc[f, i].T.astype(jnp.bfloat16)

    for stage in range(2):
        for jj in range(2):
            def drain(slot, carry):
                remote(stage, jj, slot).wait_send()
                return carry
            lax.fori_loop(1, PEERS, drain, 0)
    for jj in range(2):
        for dx in (1, 2, 3):
            z_copy(jj, dx).wait_send()


def local(u_data, u_basis, v_basis, ranks, time_mask):
    times = time_mask.shape[0]
    table = jnp.asarray(lag_table(times))
    anywhere = pl.BlockSpec(memory_space=pl.ANY)
    bf16, f32 = jnp.bfloat16, jnp.float32
    return pl.pallas_call(
        kernel,
        out_shape=jax.ShapeDtypeStruct(u_data.shape, bf16),
        in_specs=[anywhere] * 6,
        out_specs=pl.BlockSpec(memory_space=pltpu.VMEM),
        scratch_shapes=[
            pltpu.VMEM(u_data.shape, bf16),
            pltpu.VMEM(u_basis.shape, bf16),
            pltpu.VMEM(v_basis.shape, bf16),
            pltpu.SMEM(ranks.shape, jnp.int32),
            pltpu.VMEM(time_mask.shape, jnp.int32),
            pltpu.VMEM(table.shape, f32),
            pltpu.VMEM((2, 2, 2 * TILE, WIDTH), bf16),
            pltpu.VMEM((LAGS, 2, 64, 128), f32),
            pltpu.VMEM((2, 2, PEERS, 2 * PAIR, WIDTH), bf16),
            pltpu.VMEM((2, 2, PEERS, 2 * PAIR, WIDTH), bf16),
            pltpu.VMEM((2, 2, WIDTH, TILE), bf16),
            pltpu.VMEM((2, 3, 2, WIDTH, TILE), bf16),
            pltpu.VMEM((2, WIDTH, TILE), f32),
            pltpu.VMEM((2, 2, WIDTH, TILE), f32),
            pltpu.SemaphoreType.DMA((4,)),
            pltpu.SemaphoreType.DMA((2, PEERS)),
            pltpu.SemaphoreType.DMA((2, PEERS)),
            pltpu.SemaphoreType.DMA((2, 2, PEERS)),
            pltpu.SemaphoreType.DMA((2, 2, PEERS)),
            pltpu.SemaphoreType.DMA((2, 3)),
            pltpu.SemaphoreType.DMA((2, 3)),
        ],
        compiler_params=pltpu.CompilerParams(
            collective_id=0, has_side_effects=True, vmem_limit_bytes=63 * 1024 * 1024
        ),
        name="fused",
    )(u_data, u_basis, v_basis, ranks, time_mask, table)


def solution(mesh):
    placed = (
        P("freq", "tile", None),
        P("freq", "tile", None, None, None, None),
        P("freq", None, "tile", None, None, None),
        P("freq", None, None),
        P(),
    )
    return jax.shard_map(
        local, mesh=mesh, in_specs=placed, out_specs=P("freq", "tile", None), check_vma=False
    )
```

profile of v0, /device:TPU:1, one launch (start us, length us, event | category | flops | bytes accessed | tf_op | source)
XLA Modules:
  0.0 71.1 jit_solution(11869879857612748418)
XLA Ops:
  0.0 69.4 %fused.1 = bf16[2,512,128]{2,1,0:T(8,128)(2,1)} custom-call(bf16[2,512,128]{2,1,0:T(8,128)(2,1)} %u_hbm.1, bf16[2,2,64,2,48,256]{5,4,3,2,1,0:T(8,128)(2,1)} %ub_hbm.1, bf16[2,64,2,2,48,256]{5,4,3,2,1,0:T(8,128)(2,1)} %vb_hbm.1, s32[2,64,64]{2,1,0:T(8,128)} %ranks_hbm.1, s32[64,64]{1,0:T(8,128)} %mask_hbm.1, f32[64,128]{1,0:T(8,128)} %constant.2.clone.table_hbm), custom_call_target="tpu_custom_call" | custom-call | tf_op jit(solution)/shard_map/fused/pallas_call | solution.py:361
  69.4 1.7 %copy.8 = bf16[2,512,128]{2,1,0:T(8,128)(2,1)} copy(bf16[2,512,128]{2,1,0:T(8,128)(2,1)} %fused.1) | data formatting | bytes 524288
where the time goes:
time: 71.2 us; the launch traced here: 71.1 us
  Pallas kernels  69.4 us (97%)
  local copies, waits for them, and re-layouts  1.67 us (2%)
    pallas_call x1, Pallas kernels, local(): pl.pallas_call(kernel, out_shape=jax.ShapeDtypeStruct(u_data.shape, bf16)...  69.4 us
    unnamed x1, local copies, waits for them, and re-layouts  1.67 us

commit v1 on v0

v1 whole, which is shorter than its diff:
```python
import math

import jax
import jax.numpy as jnp
import numpy as np
from jax import lax
from jax.experimental import pallas as pl
from jax.experimental.pallas import tpu as pltpu
from jax.sharding import PartitionSpec as P

MESH = pl.DeviceIdType.MESH
PEERS = 32
GROUP = 4
GROUPS = PEERS // GROUP
SLOTS = 48
PAIR = 56
WIDTH = 128
TILE = 256
LAGS = 15


def lag_table(times):
    table = np.zeros((times, 128), np.float32)
    t = np.arange(times)
    for lag in range(-7, 8):
        angle = 2.0 * math.pi * ((lag * t) % times) / times
        table[:, 2 * (lag + 7)] = np.cos(angle) / times
        table[:, 2 * (lag + 7) + 1] = np.sin(angle) / times
    return table


SELF = PEERS - 1


def quot(a, b):
    return a // b if isinstance(a, int) else lax.div(a, b)


def mod(a, b):
    return a % b if isinstance(a, int) else lax.rem(a, b)


def offset(group, k):
    half = quot(group, 4)
    return mod(1 + group, 4), 2 + half if k < 2 else 1 - half, 1 - k % 2


def flip8(x):
    rows = lax.broadcasted_iota(jnp.int32, (8, WIDTH), 0)
    return jnp.take_along_axis(x, 7 - rows, axis=0)


def pack(first, second, rank):
    rows = lax.broadcasted_iota(jnp.int32, (8, WIDTH), 0)
    parts = [first[0:8]]
    for v in range(1, 6):
        other = flip8(second[8 * (6 - v) : 8 * (6 - v) + 8])
        parts.append(jnp.where(rows + 8 * v < rank, first[8 * v : 8 * v + 8], other))
    parts.append(flip8(second[0:8]))
    return parts


def unpack(packed, rank):
    rows = lax.broadcasted_iota(jnp.int32, (8, WIDTH), 0)
    first, second = [], []
    for v in range(6):
        first.append(jnp.where(rows + 8 * v < rank, packed[v], 0.0))
        second.append(jnp.where(rows + 8 * v < PAIR - rank, flip8(packed[6 - v]), 0.0))
    return jnp.concatenate(first, axis=0), jnp.concatenate(second, axis=0)


def turned(x):
    lanes = lax.broadcasted_iota(jnp.int32, x.shape, 1)
    rolled = pltpu.roll(x, WIDTH // 2, 1)
    return jnp.where(lanes < WIDTH // 2, -rolled, rolled)


def kernel(
    u_hbm, ub_hbm, vb_hbm, ranks_hbm, mask_hbm, table_hbm, out_ref,
    u_buf, ub, vb, ranks, mask, table, weights, lags, prod, side, turns,
    send, recv, z_send, z_recv, z_acc, r_acc,
    in_sem, u_sem, v_sem, send_sem, recv_sem, zs_sem, zr_sem,
):
    me = lax.axis_index("tile")
    fx = lax.axis_index("freq")
    z, y, c = quot(me, 8), mod(quot(me, 2), 4), mod(me, 2)
    zs = [mod(z + d, 4) * 8 for d in range(4)]
    ys = [mod(y + d, 4) * 2 for d in range(4)]
    cs = [c, 1 - c]
    xs = [mod(fx + d, 4) for d in range(4)]
    scope = jax.named_scope

    barrier = pltpu.get_barrier_semaphore()
    for slot in range(SELF):
        dz, dy, dc = offset(slot // GROUP, slot % GROUP)
        pl.semaphore_signal(
            barrier, inc=1, device_id={"tile": zs[dz] + ys[dy] + cs[dc]}, device_id_type=MESH
        )
    for dx in (1, 2, 3):
        pl.semaphore_signal(barrier, inc=1, device_id={"freq": xs[dx]}, device_id_type=MESH)

    copies = [
        pltpu.make_async_copy(u_hbm, u_buf, in_sem.at[0]),
        pltpu.make_async_copy(ranks_hbm, ranks, in_sem.at[1]),
        pltpu.make_async_copy(mask_hbm, mask, in_sem.at[2]),
        pltpu.make_async_copy(table_hbm, table, in_sem.at[3]),
    ]

    def u_copy(dz):
        cut = pl.ds(pl.multiple_of(2 * zs[dz], 16), 16)
        return pltpu.make_async_copy(ub_hbm.at[:, :, cut], ub.at[:, :, cut], u_sem.at[dz])

    def v_copy(dz):
        cut = pl.ds(pl.multiple_of(2 * zs[(4 - dz) % 4], 16), 16)
        return pltpu.make_async_copy(vb_hbm.at[:, cut], vb.at[:, cut], v_sem.at[dz])

    copies[0].start()
    copies[1].start()
    for dz in (1, 2, 3, 0):
        u_copy(dz).start()
    copies[2].start()
    copies[3].start()

    def targets(group):
        spots = []
        for k in range(GROUP):
            dz, dy, dc = offset(group, k)
            spots.append(mod(z + dz, 4) * 8 + mod(y + dy, 4) * 2 + cs[dc])
        return spots

    def sources(group):
        spots = []
        for k in range(GROUP):
            dz, dy, dc = offset(group, k)
            spots.append(mod(z + 4 - dz, 4) * 8 + mod(y + 4 - dy, 4) * 2 + cs[dc])
        return spots

    def dispatch(stage, jj, group, count=GROUP):
        where = targets(group)
        for k in range(count):
            slot = GROUP * group + k
            pltpu.make_async_remote_copy(
                src_ref=send.at[stage, jj, slot],
                dst_ref=recv.at[stage, jj, slot],
                send_sem=send_sem.at[stage, jj],
                recv_sem=recv_sem.at[stage, jj, group],
                device_id={"tile": where[k]},
                device_id_type=MESH,
            ).start()

    def bulk(stage, jj, first, count, sem):
        cut = pl.ds(first, count)
        return pltpu.make_async_copy(send.at[stage, jj, cut], recv.at[stage, jj, cut], sem)

    def arrive(stage, jj, group, count=GROUP):
        bulk(stage, jj, GROUP * group, count, recv_sem.at[stage, jj, group]).wait()

    with scope("u_wait"):
        copies[0].wait()
    for f in range(2):
        for i in range(2):
            x = u_buf[f, 256 * i : 256 * i + 256, :]
            weights[f, i, 0:256, :] = x
            weights[f, i, 256:512, :] = (-turned(x.astype(jnp.float32))).astype(jnp.bfloat16)
    copies[1].wait()

    def multiply(group, tile, weight):
        where = targets(group)
        for i in range(2):
            for f in range(2):
                tiles = [tile(f, i, d) for d in where]
                real = jnp.concatenate([t[0] for t in tiles], axis=0)
                imag = jnp.concatenate([t[1] for t in tiles], axis=0)
                lhs = jnp.concatenate([real, imag], axis=1)
                prod[i, f] = jnp.dot(lhs, weight(f, i), preferred_element_type=jnp.float32)

    def emit(stage, jj, group, rank):
        where = targets(group)
        for k in range(GROUP):
            cut = slice(48 * k, 48 * k + 48)
            parts = []
            for i in range(2):
                parts += pack(prod[i, 0, cut], prod[i, 1, cut], rank(i, where[k]))
            send[stage, jj, GROUP * group + k] = jnp.concatenate(parts, axis=0).astype(jnp.bfloat16)

    def coefficients(stage, jj, tile, weight, rank, before=None, between=None, paced=False):
        multiply(0, tile, weight)
        if before is not None:
            before(1)
        emit(stage, jj, 0, rank)
        multiply(1, tile, weight)

        def step(group, carry):
            if not paced:
                dispatch(stage, jj, group - 2)
            emit(stage, jj, group - 1, rank)
            multiply(group, tile, weight)
            return carry

        first = 2
        if before is not None:
            before(2)
            step(2, 0)
            before(3)
            first = 3
        if between is not None:
            lax.fori_loop(first, GROUPS // 2 + 1, step, 0)
            first = GROUPS // 2 + 1
            between()
        lax.fori_loop(first, GROUPS, step, 0)
        if not paced:
            dispatch(stage, jj, GROUPS - 2)
        emit(stage, jj, GROUPS - 1, rank)
        if not paced:
            dispatch(stage, jj, GROUPS - 1, GROUP - 1)

    def adjoint(jj, **marks):
        coefficients(
            0, jj,
            lambda f, i, d: ub[f, i, 2 * d + jj],
            lambda f, i: weights[f, i],
            lambda i, d: ranks[0, 2 * me + i, 2 * d + jj],
            **marks,
        )

    def forward(jj, **marks):
        coefficients(
            1, jj,
            lambda f, i, d: vb[f, 2 * d + i, jj],
            lambda f, i: weights[f, 0],
            lambda i, d: ranks[0, 2 * d + i, 2 * me + jj],
            **marks,
        )

    def loaded(group):
        if group == 1:
            u_copy(2).wait()
        elif group == 2:
            u_copy(3).wait()
            with scope("barrier"):
                pl.semaphore_wait(barrier, PEERS - 1 + 3)
        else:
            u_copy(0).wait()
            for dz in (1, 2, 3, 0):
                v_copy(dz).start()

    with scope("adj0"):
        u_copy(1).wait()
        adjoint(0, before=loaded)
    with scope("adj1"):
        adjoint(1, paced=True)

    copies[2].wait()
    copies[3].wait()
    kept = mask[...].astype(jnp.float32)
    mixing = lax.dot_general(
        kept, table[...], (((0,), (0,)), ((), ())),
        precision=lax.Precision.HIGHEST, preferred_element_type=jnp.float32,
    )
    for lag in range(LAGS):
        for part in range(2):
            column = mixing[:, 2 * lag + part : 2 * lag + part + 1]
            lags[lag, part] = jnp.broadcast_to(column, (64, 128))

    def crossed(x):
        half = WIDTH // 2
        return jnp.concatenate([-x[half:], x[:half]], axis=0)

    def opened(stage, jj, slot, rank):
        block = (send if slot is None else recv)[stage, jj, SELF if slot is None else slot]
        block = block.astype(jnp.float32)
        pairs = []
        for i in range(2):
            pieces = [block[56 * i + 8 * v : 56 * i + 8 * v + 8] for v in range(7)]
            pairs.append(unpack(pieces, rank(i)))
        return pairs

    def slot_of(group, k, last):
        return None if last and k == GROUP - 1 else GROUP * group + k

    def take(jj, group, last=False):
        whence = sources(group)
        stacks = [[], []]
        for k in range(GROUP):
            pairs = opened(
                0, jj, slot_of(group, k, last), lambda i: ranks[0, 2 * whence[k] + i, 2 * me + jj]
            )
            for i in range(2):
                for f in range(2):
                    stacks[f].append(pairs[i][f].astype(jnp.bfloat16))
        for f in range(2):
            side[f] = jnp.concatenate(stacks[f], axis=0).T

    def add(jj, group):
        whence = sources(group)
        for f in range(2):
            held = side[f]
            lhs = jnp.concatenate([held, crossed(held)], axis=1)
            rhs = jnp.concatenate(
                [vb[f, 2 * d + i, jj, c] for c in range(2) for d in whence for i in range(2)], axis=0
            )
            z_acc[f] += jnp.dot(lhs, rhs, preferred_element_type=jnp.float32)

    def take_back(jj, group, last=False):
        whence = sources(group)
        stacks = [[[], []], [[], []]]
        for k in range(GROUP):
            pairs = opened(
                1, jj, slot_of(group, k, last), lambda i: ranks[0, 2 * me + i, 2 * whence[k] + jj]
            )
            for i in range(2):
                for f in range(2):
                    stacks[f][i].append(pairs[i][f].astype(jnp.bfloat16))
        for f in range(2):
            for i in range(2):
                turns[f, i] = jnp.concatenate(stacks[f][i], axis=0).T

    def add_back(jj, group):
        whence = sources(group)
        for f in range(2):
            for i in range(2):
                held = turns[f, i]
                total = r_acc[f, i]
                for c, lhs in enumerate((held, crossed(held))):
                    rhs = jnp.concatenate([ub[f, i, 2 * d + jj, c] for d in whence], axis=0)
                    total = total + jnp.dot(lhs, rhs, preferred_element_type=jnp.float32)
                r_acc[f, i] = total

    def gather(stage, jj, first, stop, then=None):
        unpack_group, add_group = ((take, add), (take_back, add_back))[stage]
        if first == 0:
            arrive(stage, jj, 0)
            if then is not None:
                dispatch(*then, 0)
            unpack_group(jj, 0)
            first = 1

        def step(group, carry):
            arrive(stage, jj, group)
            if then is not None:
                dispatch(*then, group)
            add_group(jj, group - 1)
            unpack_group(jj, group)
            return carry

        lax.fori_loop(first, min(stop, GROUPS - 1), step, 0)
        if stop == GROUPS:
            arrive(stage, jj, GROUPS - 1, GROUP - 1)
            if then is not None:
                dispatch(*then, GROUPS - 1, GROUP - 1)
            add_group(jj, GROUPS - 2)
            unpack_group(jj, GROUPS - 1, True)
            add_group(jj, GROUPS - 1)

    def clear():
        z_acc[...] = jnp.zeros_like(z_acc)

    def z_copy(jj, dx):
        return pltpu.make_async_remote_copy(
            src_ref=z_send.at[jj],
            dst_ref=z_recv.at[jj, dx - 1],
            send_sem=zs_sem.at[jj, dx - 1],
            recv_sem=zr_sem.at[jj, dx - 1],
            device_id={"freq": xs[dx]},
            device_id_type=MESH,
        )

    def share(jj):
        z_send[jj] = z_acc[...].astype(jnp.bfloat16)
        for dx in (2, 1, 3):
            z_copy(jj, dx).start()

    def mix(jj):
        with scope(f"mixwait{jj}"):
            for dx in (1, 3, 2):
                z_copy(jj, dx).wait_recv()
        for f in range(2):
            for h in range(2):
                cut = slice(128 * h, 128 * h + 128)
                real = jnp.zeros((64, 128), jnp.float32)
                imag = jnp.zeros((64, 128), jnp.float32)
                for dx in range(4):
                    for g in range(2):
                        held = z_send.at[jj] if dx == 0 else z_recv.at[jj, dx - 1]
                        zr = held[g, 0:64, cut].astype(jnp.float32)
                        zi = held[g, 64:128, cut].astype(jnp.float32)
                        lag = 2 * (xs[(4 - dx) % 4] - fx) + g - f + 7
                        cr = lags[lag, 0]
                        ci = lags[lag, 1]
                        real += cr * zr - ci * zi
                        imag += cr * zi + ci * zr
                straight = jnp.concatenate([real, imag], axis=0)
                swapped = jnp.concatenate([imag, -real], axis=0)
                weights[f, 0, 128 * h : 128 * h + 128, :] = straight.T.astype(jnp.bfloat16)
                weights[f, 0, 256 + 128 * h : 384 + 128 * h, :] = swapped.T.astype(jnp.bfloat16)

    clear()
    r_acc[...] = jnp.zeros_like(r_acc)
    for dz in (1, 2, 3, 0):
        v_copy(dz).wait()
    with scope("gather0"):
        gather(0, 0, 0, GROUPS, then=(0, 1))
    with scope("share0"):
        share(0)
        clear()
    with scope("gather1a"):
        gather(0, 1, 0, 3)

    def rest():
        with scope("gather1b"):
            gather(0, 1, 3, GROUPS)
        with scope("share1"):
            share(1)

    with scope("mix0"):
        mix(0)
    with scope("forward0"):
        forward(0)
    rest()
    with scope("finish0a"):
        pass
    with scope("mix1"):
        mix(1)
    with scope("forward1"):
        forward(1)
    with scope("finish0b"):
        gather(1, 0, 0, GROUPS)
    with scope("finish1"):
        gather(1, 1, 0, GROUPS)
    with scope("tail"):
        for f in range(2):
            for i in range(2):
                out_ref[f, 256 * i : 256 * i + 256, :] = r_acc[f, i].T.astype(jnp.bfloat16)
        for stage in range(2):
            for jj in range(2):
                bulk(stage, jj, 0, SELF, send_sem.at[stage, jj]).wait()
        for jj in range(2):
            for dx in (1, 2, 3):
                z_copy(jj, dx).wait_send()


def local(u_data, u_basis, v_basis, ranks, time_mask):
    times = time_mask.shape[0]
    table = jnp.asarray(lag_table(times))
    anywhere = pl.BlockSpec(memory_space=pl.ANY)
    bf16, f32 = jnp.bfloat16, jnp.float32
    return pl.pallas_call(
        kernel,
        out_shape=jax.ShapeDtypeStruct(u_data.shape, bf16),
        in_specs=[anywhere] * 6,
        out_specs=pl.BlockSpec(memory_space=pltpu.VMEM),
        scratch_shapes=[
            pltpu.VMEM(u_data.shape, bf16),
            pltpu.VMEM(u_basis.shape, bf16),
            pltpu.VMEM(v_basis.shape, bf16),
            pltpu.SMEM(ranks.shape, jnp.int32),
            pltpu.VMEM(time_mask.shape, jnp.int32),
            pltpu.VMEM(table.shape, f32),
            pltpu.VMEM((2, 2, 2 * TILE, WIDTH), bf16),
            pltpu.VMEM((LAGS, 2, 64, 128), f32),
            pltpu.VMEM((2, 2, GROUP * SLOTS, WIDTH), f32),
            pltpu.VMEM((2, WIDTH, 2 * GROUP * SLOTS), bf16),
            pltpu.VMEM((2, 2, WIDTH, GROUP * SLOTS), bf16),
            pltpu.VMEM((2, 2, PEERS, 2 * PAIR, WIDTH), bf16),
            pltpu.VMEM((2, 2, PEERS, 2 * PAIR, WIDTH), bf16),
            pltpu.VMEM((2, 2, WIDTH, TILE), bf16),
            pltpu.VMEM((2, 3, 2, WIDTH, TILE), bf16),
            pltpu.VMEM((2, WIDTH, TILE), f32),
            pltpu.VMEM((2, 2, WIDTH, TILE), f32),
            pltpu.SemaphoreType.DMA((4,)),
            pltpu.SemaphoreType.DMA((4,)),
            pltpu.SemaphoreType.DMA((4,)),
            pltpu.SemaphoreType.DMA((2, 2)),
            pltpu.SemaphoreType.DMA((2, 2, GROUPS)),
            pltpu.SemaphoreType.DMA((2, 3)),
            pltpu.SemaphoreType.DMA((2, 3)),
        ],
        compiler_params=pltpu.CompilerParams(
            collective_id=0, has_side_effects=True, vmem_limit_bytes=63 * 1024 * 1024
        ),
        name="fused",
    )(u_data, u_basis, v_basis, ranks, time_mask, table)


def solution(mesh):
    placed = (
        P("freq", "tile", None),
        P("freq", "tile", None, None, None, None),
        P("freq", None, "tile", None, None, None),
        P("freq", None, None),
        P(),
    )
    return jax.shard_map(
        local, mesh=mesh, in_specs=placed, out_specs=P("freq", "tile", None), check_vma=False
    )
```

time: 71.2 us -> 61.4 us (0.86)
  Pallas kernels: 69.4 us -> 59.6 us
    pallas_call x1, Pallas kernels: 69.4 us -> 59.6 us  [local(): pl.pallas_call(kernel, out_shape=jax.ShapeDtypeStruct(u_data.shape, bf16)...]
where the time goes in v1:
time: 61.4 us; the launch traced here: 61.3 us
  Pallas kernels  59.6 us (97%)
  local copies, waits for them, and re-layouts  1.67 us (3%)
    pallas_call x1, Pallas kernels, local(): pl.pallas_call(kernel, out_shape=jax.ShapeDtypeStruct(u_data.shape, bf16)...  59.6 us
    unnamed x1, local copies, waits for them, and re-layouts  1.67 us

profile of v1, /device:TPU:1, one launch (start us, length us, event | category | flops | bytes accessed | tf_op | source)
XLA Modules:
  0.0 61.3 jit_solution(5048791141730553441)
XLA Ops:
  0.0 59.6 %fused.1 = bf16[2,512,128]{2,1,0:T(8,128)(2,1)} custom-call(bf16[2,512,128]{2,1,0:T(8,128)(2,1)} %u_hbm.1, bf16[2,2,64,2,48,256]{5,4,3,2,1,0:T(8,128)(2,1)} %ub_hbm.1, bf16[2,64,2,2,48,256]{5,4,3,2,1,0:T(8,128)(2,1)} %vb_hbm.1, s32[2,64,64]{2,1,0:T(8,128)} %ranks_hbm.1, s32[64,64]{1,0:T(8,128)} %mask_hbm.1, f32[64,128]{1,0:T(8,128)} %constant.2.clone.table_hbm), custom_call_target="tpu_custom_call" | custom-call | tf_op jit(solution)/shard_map/fused/pallas_call | solution.py:447
  59.6 1.7 %copy.8 = bf16[2,512,128]{2,1,0:T(8,128)(2,1)} copy(bf16[2,512,128]{2,1,0:T(8,128)(2,1)} %fused.1) | data formatting | bytes 524288

commit v2 on v1

v2 whole, which is shorter than its diff:
```python
import math

import jax
import jax.numpy as jnp
import numpy as np
from jax import lax
from jax.experimental import pallas as pl
from jax.experimental.pallas import tpu as pltpu
from jax.sharding import PartitionSpec as P

MESH = pl.DeviceIdType.MESH
PEERS = 32
LEAD = 7
GROUP = 4
GROUPS = PEERS // GROUP
SLOTS = 48
PAIR = 56
WIDTH = 128
TILE = 256
LAGS = 15


def lag_table(times):
    table = np.zeros((times, 128), np.float32)
    t = np.arange(times)
    for lag in range(-7, 8):
        angle = 2.0 * math.pi * ((lag * t) % times) / times
        table[:, 2 * (lag + 7)] = np.cos(angle) / times
        table[:, 2 * (lag + 7) + 1] = np.sin(angle) / times
    return table


SELF = PEERS - 1


def quot(a, b):
    return a // b if isinstance(a, int) else lax.div(a, b)


def mod(a, b):
    return a % b if isinstance(a, int) else lax.rem(a, b)


def offset(group, k):
    half = quot(group, 4)
    return mod(1 + group, 4), 2 + half if k < 2 else 1 - half, 1 - k % 2


def flip8(x):
    rows = lax.broadcasted_iota(jnp.int32, (8, WIDTH), 0)
    return jnp.take_along_axis(x, 7 - rows, axis=0)


def pack(first, second, rank):
    rows = lax.broadcasted_iota(jnp.int32, (8, WIDTH), 0)
    parts = [first[0:8]]
    for v in range(1, 6):
        other = flip8(second[8 * (6 - v) : 8 * (6 - v) + 8])
        parts.append(jnp.where(rows + 8 * v < rank, first[8 * v : 8 * v + 8], other))
    parts.append(flip8(second[0:8]))
    return parts


def unpack(packed, rank):
    rows = lax.broadcasted_iota(jnp.int32, (8, WIDTH), 0)
    first, second = [], []
    for v in range(6):
        first.append(jnp.where(rows + 8 * v < rank, packed[v], 0.0))
        second.append(jnp.where(rows + 8 * v < PAIR - rank, flip8(packed[6 - v]), 0.0))
    return jnp.concatenate(first, axis=0), jnp.concatenate(second, axis=0)


def interleaved(x):
    part = lax.broadcasted_iota(jnp.int32, x.shape, 1) // 32
    by32, by64, by96 = (pltpu.roll(x, shift, 1) for shift in (32, 64, 96))
    straight = jnp.where(part == 1, by96, jnp.where(part == 2, by32, x))
    swapped = jnp.where(part == 0, by64, jnp.where(part == 1, -by32, jnp.where(part == 2, by96, -by64)))
    return straight, swapped


def crossed(x):
    rows = []
    for at in range(0, x.shape[0], 64):
        rows += [-x[at + 32 : at + 64], x[at : at + 32]]
    return jnp.concatenate(rows, axis=0)


def kernel(
    u_hbm, ub_hbm, vb_hbm, ranks_hbm, mask_hbm, table_hbm, out_ref,
    u_buf, ub, vb, ranks, mask, table, weights, lags, prod, side, turns, mixed,
    send_a, recv_a, send_b, recv_b, z_send, z_recv, z_acc, r_acc,
    in_sem, u_sem, v_sem, sent_a, got_a, sent_b, got_b, zs_sem, zr_sem,
):
    me = lax.axis_index("tile")
    fx = lax.axis_index("freq")
    z, y, c = quot(me, 8), mod(quot(me, 2), 4), mod(me, 2)
    zs = [mod(z + d, 4) * 8 for d in range(4)]
    ys = [mod(y + d, 4) * 2 for d in range(4)]
    cs = [c, 1 - c]
    xs = [mod(fx + d, 4) for d in range(4)]
    scope = jax.named_scope

    barrier = pltpu.get_barrier_semaphore()
    for slot in range(SELF):
        dz, dy, dc = offset(slot // GROUP, slot % GROUP)
        pl.semaphore_signal(
            barrier, inc=1, device_id={"tile": zs[dz] + ys[dy] + cs[dc]}, device_id_type=MESH
        )
    for dx in (1, 2, 3):
        pl.semaphore_signal(barrier, inc=1, device_id={"freq": xs[dx]}, device_id_type=MESH)

    copies = [
        pltpu.make_async_copy(u_hbm, u_buf, in_sem.at[0]),
        pltpu.make_async_copy(ranks_hbm, ranks, in_sem.at[1]),
        pltpu.make_async_copy(mask_hbm, mask, in_sem.at[2]),
        pltpu.make_async_copy(table_hbm, table, in_sem.at[3]),
    ]

    def u_copy(dz):
        cut = pl.ds(pl.multiple_of(2 * zs[dz], 16), 16)
        return pltpu.make_async_copy(ub_hbm.at[:, :, cut], ub.at[:, :, cut], u_sem.at[dz])

    def v_copy(dz):
        cut = pl.ds(pl.multiple_of(2 * zs[(4 - dz) % 4], 16), 16)
        return pltpu.make_async_copy(vb_hbm.at[:, cut], vb.at[:, cut], v_sem.at[dz])

    copies[0].start()
    copies[1].start()
    for dz in (1, 2, 3, 0):
        u_copy(dz).start()
    copies[2].start()
    copies[3].start()

    def targets(group):
        spots = []
        for k in range(GROUP):
            dz, dy, dc = offset(group, k)
            spots.append(mod(z + dz, 4) * 8 + mod(y + dy, 4) * 2 + cs[dc])
        return spots

    def sources(group):
        spots = []
        for k in range(GROUP):
            dz, dy, dc = offset(group, k)
            spots.append(mod(z + 4 - dz, 4) * 8 + mod(y + 4 - dy, 4) * 2 + cs[dc])
        return spots

    def ends(chunk):
        at = chunk[1]
        if chunk[0] == 0:
            return send_a.at[at], recv_a.at[at], sent_a.at[at], got_a.at[at]
        return send_b.at[at], recv_b.at[at], sent_b.at[at], got_b.at[at]

    def dispatch(chunk, group, count=GROUP):
        source, landing, sent, got = ends(chunk)
        where = targets(group)
        for k in range(*count) if isinstance(count, tuple) else range(count):
            slot = GROUP * group + k
            pltpu.make_async_remote_copy(
                src_ref=source.at[slot],
                dst_ref=landing.at[slot],
                send_sem=sent,
                recv_sem=got.at[group],
                device_id={"tile": where[k]},
                device_id_type=MESH,
            ).start()

    def dispatch_next(number):
        @pl.when(number < 4 * GROUPS)
        def _():
            chunk, group = (0, lax.div(number, GROUPS)), lax.rem(number, GROUPS)
            dispatch(chunk, group, GROUP - 1)

            @pl.when(group < GROUPS - 1)
            def _():
                dispatch(chunk, group, (GROUP - 1, GROUP))

    def arrive(chunk, group, count=GROUP):
        source, landing, _, got = ends(chunk)
        cut = pl.ds(GROUP * group, count)
        pltpu.make_async_copy(source.at[cut], landing.at[cut], got.at[group]).wait()

    def drain(chunk):
        source, landing, sent, _ = ends(chunk)
        cut = pl.ds(0, SELF)
        pltpu.make_async_copy(source.at[cut], landing.at[cut], sent).wait()

    with scope("u_wait"):
        copies[0].wait()
    for f in range(2):
        for i in range(2):
            x = u_buf[f, 256 * i : 256 * i + 256, :].astype(jnp.float32)
            straight, swapped = interleaved(x)
            weights[f, i, 0:256, :] = straight.astype(jnp.bfloat16)
            weights[f, i, 256:512, :] = swapped.astype(jnp.bfloat16)
    copies[1].wait()

    def multiply(group, tile, weight):
        where = targets(group)
        for i in range(2):
            for f in range(2):
                tiles = [tile(f, i, d) for d in where]
                real = jnp.concatenate([t[0] for t in tiles], axis=0)
                imag = jnp.concatenate([t[1] for t in tiles], axis=0)
                lhs = jnp.concatenate([real, imag], axis=1)
                prod[i, f] = jnp.dot(lhs, weight(f, i), preferred_element_type=jnp.float32)

    def emit(stage, jj, group, rank):
        where = targets(group)
        low = lax.broadcasted_iota(jnp.int32, (8, WIDTH), 1) < WIDTH // 2
        for k in range(GROUP):
            slot = GROUP * group + k
            cut = slice(48 * k, 48 * k + 48)
            top, bottom = (pack(prod[i, 0, cut], prod[i, 1, cut], rank(i, where[k])) for i in range(2))
            if stage == 1:
                send_b[jj, slot] = jnp.concatenate(top + bottom, axis=0).astype(jnp.bfloat16)
                continue
            pairs = list(zip(top, bottom))
            left = [jnp.where(low, t, pltpu.roll(b, WIDTH // 2, 1)) for t, b in pairs]
            right = [jnp.where(low, pltpu.roll(t, WIDTH // 2, 1), b) for t, b in pairs]
            send_a[2 * jj, slot] = jnp.concatenate(left, axis=0).astype(jnp.bfloat16)
            send_a[2 * jj + 1, slot] = jnp.concatenate(right, axis=0).astype(jnp.bfloat16)

    def coefficients(stage, jj, tile, weight, rank, before=None, chunk=None):
        multiply(0, tile, weight)
        emit(stage, jj, 0, rank)
        if before is not None:
            before(1)
            dispatch(chunk, 0)
        multiply(1, tile, weight)

        def step(group, carry):
            if chunk is not None:
                dispatch(chunk, group - 2)
            emit(stage, jj, group - 1, rank)
            multiply(group, tile, weight)
            return carry

        first = 2
        if before is not None:
            before(2)
            emit(stage, jj, 1, rank)
            multiply(2, tile, weight)
            before(3)
            first = 3
        lax.fori_loop(first, GROUPS, step, 0)
        if chunk is not None:
            dispatch(chunk, GROUPS - 2)
        emit(stage, jj, GROUPS - 1, rank)
        if chunk is not None:
            dispatch(chunk, GROUPS - 1, GROUP - 1)

    def adjoint(jj, **marks):
        coefficients(
            0, jj,
            lambda f, i, d: ub[f, i, 2 * d + jj],
            lambda f, i: weights[f, i],
            lambda i, d: ranks[0, 2 * me + i, 2 * d + jj],
            **marks,
        )

    def forward(jj):
        coefficients(
            1, jj,
            lambda f, i, d: vb[f, 2 * d + i, jj],
            lambda f, i: weights[f, 0],
            lambda i, d: ranks[0, 2 * d + i, 2 * me + jj],
            chunk=(1, jj),
        )

    def loaded(group):
        if group == 1:
            with scope("barrier"):
                pl.semaphore_wait(barrier, PEERS - 1 + 3)
            u_copy(2).wait()
        elif group == 2:
            u_copy(3).wait()
        else:
            u_copy(0).wait()
            for dz in (1, 2, 3, 0):
                v_copy(dz).start()

    with scope("adj0"):
        u_copy(1).wait()
        adjoint(0, before=loaded, chunk=(0, 0))
        for group in range(LEAD):
            dispatch((0, 1), group)
    with scope("adj1"):
        adjoint(1)

    copies[2].wait()
    copies[3].wait()
    kept = mask[...].astype(jnp.float32)
    mixing = lax.dot_general(
        kept, table[...], (((0,), (0,)), ((), ())),
        precision=lax.Precision.HIGHEST, preferred_element_type=jnp.float32,
    )
    for lag in range(LAGS):
        for part in range(2):
            column = mixing[:, 2 * lag + part : 2 * lag + part + 1]
            lags[lag, part] = jnp.broadcast_to(column, (64, 128))

    def pieces_of(block, start):
        return [block[start + 8 * v : start + 8 * v + 8] for v in range(7)]

    def slot_of(group, k, last):
        return None if last and k == GROUP - 1 else GROUP * group + k

    def take(chunk, group, last=False):
        jj = chunk[1] // 2
        whence = sources(group)
        low = lax.broadcasted_iota(jnp.int32, (8, WIDTH), 1) < WIDTH // 2
        stacks = [[], []]
        for k in range(GROUP):
            slot = slot_of(group, k, last)
            block = (send_a if slot is None else recv_a)[chunk[1], SELF if slot is None else slot]
            rank = jnp.where(low, *(ranks[0, 2 * whence[k] + i, 2 * me + jj] for i in range(2)))
            pair = unpack(pieces_of(block.astype(jnp.float32), 0), rank)
            for f in range(2):
                stacks[f].append(pair[f].astype(jnp.bfloat16))
        for f in range(2):
            side[f] = jnp.concatenate(stacks[f], axis=0).T

    def add(chunk, group):
        jj = chunk[1] // 2
        whence = sources(group)
        for f in range(2):
            total = z_acc[f]
            for i in range(2):
                held = side[f, 64 * i : 64 * i + 64]
                for c, lhs in enumerate((held, crossed(held))):
                    rhs = jnp.concatenate([vb[f, 2 * d + i, jj, c] for d in whence], axis=0)
                    total = total + jnp.dot(lhs, rhs, preferred_element_type=jnp.float32)
            z_acc[f] = total

    def take_back(chunk, group, last=False):
        jj = chunk[1]
        whence = sources(group)
        stacks = [[[], []], [[], []]]
        for k in range(GROUP):
            slot = slot_of(group, k, last)
            block = (send_b[jj, SELF] if slot is None else recv_b[jj, slot]).astype(jnp.float32)
            for i in range(2):
                pair = unpack(pieces_of(block, PAIR * i), ranks[0, 2 * me + i, 2 * whence[k] + jj])
                for f in range(2):
                    stacks[f][i].append(pair[f].astype(jnp.bfloat16))
        for f in range(2):
            for i in range(2):
                turns[f, i] = jnp.concatenate(stacks[f][i], axis=0).T

    def add_back(chunk, group):
        jj = chunk[1]
        whence = sources(group)
        for f in range(2):
            for i in range(2):
                held = turns[f, i]
                total = r_acc[f, i]
                for c, lhs in enumerate((held, crossed(held))):
                    rhs = jnp.concatenate([ub[f, i, 2 * d + jj, c] for d in whence], axis=0)
                    total = total + jnp.dot(lhs, rhs, preferred_element_type=jnp.float32)
                r_acc[f, i] = total

    def gather(chunk, ahead=False):
        unpack_group, add_group = ((take, add), (take_back, add_back))[chunk[0]]
        arrive(chunk, 0)
        first = (chunk[1] + 1) * GROUPS + LEAD
        if ahead:
            dispatch_next(first + zero)
        unpack_group(chunk, 0)

        def step(group, carry):
            arrive(chunk, group)
            if ahead:
                dispatch_next(first + group)
            add_group(chunk, group - 1)
            unpack_group(chunk, group)
            return carry

        lax.fori_loop(1, GROUPS - 1, step, 0)
        arrive(chunk, GROUPS - 1, GROUP - 1)
        if ahead:
            dispatch_next(first + zero + GROUPS - 1)
        add_group(chunk, GROUPS - 2)
        unpack_group(chunk, GROUPS - 1, True)
        add_group(chunk, GROUPS - 1)

    zero = mod(fx, 1)

    def clear():
        z_acc[...] = jnp.zeros_like(z_acc)

    def z_copy(jj, h, dx):
        return pltpu.make_async_remote_copy(
            src_ref=z_send.at[jj, h],
            dst_ref=z_recv.at[jj, h, dx - 1],
            send_sem=zs_sem.at[jj, h, dx - 1],
            recv_sem=zr_sem.at[jj, h, dx - 1],
            device_id={"freq": xs[dx]},
            device_id_type=MESH,
        )

    def share(jj, h):
        z_send[jj, h] = z_acc[...].astype(jnp.bfloat16)
        for dx in (2, 1, 3):
            z_copy(jj, h, dx).start()
        clear()

    def mix(jj, h):
        with scope(f"mixwait{jj}{h}"):
            for dx in (1, 3, 2):
                z_copy(jj, h, dx).wait_recv()
        rows = slice(32 * h, 32 * h + 32)
        for cut in (slice(0, 128), slice(128, 256)):
            total = [[jnp.zeros((32, 128), jnp.float32) for _ in range(2)] for _ in range(2)]
            for dx in range(4):
                held = z_send.at[jj, h] if dx == 0 else z_recv.at[jj, h, dx - 1]
                for g in range(2):
                    zr = held[g, 0:32, cut].astype(jnp.float32)
                    zi = held[g, 32:64, cut].astype(jnp.float32)
                    for f in range(2):
                        lag = 2 * (xs[(4 - dx) % 4] - fx) + g - f + 7
                        cr = lags[lag, 0, rows]
                        ci = lags[lag, 1, rows]
                        total[f][0] += cr * zr - ci * zi
                        total[f][1] += cr * zi + ci * zr
            for f in range(2):
                mixed[f, 64 * h : 64 * h + 32, cut] = total[f][0]
                mixed[f, 64 * h + 32 : 64 * h + 64, cut] = total[f][1]

    def ready():
        for f in range(2):
            both = mixed[f]
            weights[f, 0, 0:256, :] = both.T.astype(jnp.bfloat16)
            weights[f, 0, 256:512, :] = (-crossed(both)).T.astype(jnp.bfloat16)

    clear()
    r_acc[...] = jnp.zeros_like(r_acc)
    for dz in (1, 2, 3, 0):
        v_copy(dz).wait()
    with scope("gather00"):
        gather((0, 0), True)
        share(0, 0)
    with scope("gather01"):
        gather((0, 1), True)
        share(0, 1)
    with scope("gather10"):
        gather((0, 2), True)
        share(1, 0)
    with scope("mix0"):
        mix(0, 0)
        mix(0, 1)
        ready()
    with scope("forward0"):
        forward(0)
    with scope("gather11"):
        gather((0, 3))
        share(1, 1)
    with scope("mix1"):
        mix(1, 0)
        mix(1, 1)
        ready()
    with scope("forward1"):
        forward(1)
    with scope("finish0"):
        gather((1, 0))
    with scope("finish1"):
        gather((1, 1))
    with scope("tail"):
        for f in range(2):
            for i in range(2):
                x = r_acc[f, i]
                x = jnp.concatenate([x[0:32], x[64:96], x[32:64], x[96:128]], axis=0)
                out_ref[f, 256 * i : 256 * i + 256, :] = x.T.astype(jnp.bfloat16)
        for jj in range(2):
            drain((0, 2 * jj))
            drain((0, 2 * jj + 1))
            drain((1, jj))
        for jj in range(2):
            for h in range(2):
                for dx in (1, 2, 3):
                    z_copy(jj, h, dx).wait_send()


def local(u_data, u_basis, v_basis, ranks, time_mask):
    times = time_mask.shape[0]
    table = jnp.asarray(lag_table(times))
    anywhere = pl.BlockSpec(memory_space=pl.ANY)
    bf16, f32 = jnp.bfloat16, jnp.float32
    return pl.pallas_call(
        kernel,
        out_shape=pltpu.VMEM(u_data.shape, bf16),
        in_specs=[anywhere] * 6,
        out_specs=pl.BlockSpec(memory_space=pltpu.VMEM),
        scratch_shapes=[
            pltpu.VMEM(u_data.shape, bf16),
            pltpu.VMEM(u_basis.shape, bf16),
            pltpu.VMEM(v_basis.shape, bf16),
            pltpu.SMEM(ranks.shape, jnp.int32),
            pltpu.VMEM(time_mask.shape, jnp.int32),
            pltpu.VMEM(table.shape, f32),
            pltpu.VMEM((2, 2, 2 * TILE, WIDTH), bf16),
            pltpu.VMEM((LAGS, 2, 64, 128), f32),
            pltpu.VMEM((2, 2, GROUP * SLOTS, WIDTH), f32),
            pltpu.VMEM((2, WIDTH, GROUP * SLOTS), bf16),
            pltpu.VMEM((2, 2, WIDTH, GROUP * SLOTS), bf16),
            pltpu.VMEM((2, WIDTH, TILE), f32),
            pltpu.VMEM((4, PEERS, PAIR, WIDTH), bf16),
            pltpu.VMEM((4, PEERS, PAIR, WIDTH), bf16),
            pltpu.VMEM((2, PEERS, 2 * PAIR, WIDTH), bf16),
            pltpu.VMEM((2, PEERS, 2 * PAIR, WIDTH), bf16),
            pltpu.VMEM((2, 2, 2, WIDTH // 2, TILE), bf16),
            pltpu.VMEM((2, 2, 3, 2, WIDTH // 2, TILE), bf16),
            pltpu.VMEM((2, WIDTH // 2, TILE), f32),
            pltpu.VMEM((2, 2, WIDTH, TILE), f32),
            pltpu.SemaphoreType.DMA((4,)),
            pltpu.SemaphoreType.DMA((4,)),
            pltpu.SemaphoreType.DMA((4,)),
            pltpu.SemaphoreType.DMA((4,)),
            pltpu.SemaphoreType.DMA((4, GROUPS)),
            pltpu.SemaphoreType.DMA((2,)),
            pltpu.SemaphoreType.DMA((2, GROUPS)),
            pltpu.SemaphoreType.DMA((2, 2, 3)),
            pltpu.SemaphoreType.DMA((2, 2, 3)),
        ],
        compiler_params=pltpu.CompilerParams(
            collective_id=0, has_side_effects=True, vmem_limit_bytes=63 * 1024 * 1024
        ),
        name="fused",
    )(u_data, u_basis, v_basis, ranks, time_mask, table)


def solution(mesh):
    placed = (
        P("freq", "tile", None),
        P("freq", "tile", None, None, None, None),
        P("freq", None, "tile", None, None, None),
        P("freq", None, None),
        P(),
    )
    return jax.shard_map(
        local, mesh=mesh, in_specs=placed, out_specs=P("freq", "tile", None), check_vma=False
    )
```

time: 61.4 us -> 56.7 us (0.923)
  Pallas kernels: 59.6 us -> 55.9 us
  local copies, waits for them, and re-layouts: 1.67 us -> 0.71 us
    pallas_call x1, Pallas kernels: 59.6 us -> 55.9 us  [local(): pl.pallas_call(kernel, out_shape=pltpu.VMEM(u_data.shape, bf16), in_specs...]
    unnamed x1, local copies, waits for them, and re-layouts: 1.67 us -> 0.71 us
where the time goes in v2:
time: 56.7 us; the launch traced here: 56.6 us
  Pallas kernels  55.9 us (99%)
  local copies, waits for them, and re-layouts  0.71 us (1%)
    pallas_call x1, Pallas kernels, local(): pl.pallas_call(kernel, out_shape=pltpu.VMEM(u_data.shape, bf16), in_specs...  55.9 us

profile of v2, /device:TPU:1, one launch (start us, length us, event | category | flops | bytes accessed | tf_op | source)
XLA Modules:
  0.0 56.6 jit_solution(12041920000121863544)
XLA Ops:
  0.0 55.9 %fused.1 = bf16[2,512,128]{2,1,0:T(8,128)(2,1)S(1)} custom-call(bf16[2,512,128]{2,1,0:T(8,128)(2,1)} %u_hbm.1, bf16[2,2,64,2,48,256]{5,4,3,2,1,0:T(8,128)(2,1)} %ub_hbm.1, bf16[2,64,2,2,48,256]{5,4,3,2,1,0:T(8,128)(2,1)} %vb_hbm.1, s32[2,64,64]{2,1,0:T(8,128)} %ranks_hbm.1, s32[64,64]{1,0:T(8,128)} %mask_hbm.1, f32[64,128]{1,0:T(8,128)} %constant.2.clone.table_hbm), custom_call_target="tpu_custom_call" | custom-call | tf_op jit(solution)/shard_map/fused/pallas_call | solution.py:489
  55.9 0.7 %copy.8 = bf16[2,512,128]{2,1,0:T(8,128)(2,1)} copy(bf16[2,512,128]{2,1,0:T(8,128)(2,1)S(1)} %fused.1) | data formatting | bytes 524288

commit v3 on v2

--- a/solution.py
+++ b/solution.py
@@ -10,7 +10,6 @@
 
 MESH = pl.DeviceIdType.MESH
 PEERS = 32
-LEAD = 7
 GROUP = 4
 GROUPS = PEERS // GROUP
 SLOTS = 48
@@ -131,18 +130,18 @@
     copies[2].start()
     copies[3].start()
 
-    def targets(group):
+    def targets(group, hand=1):
         spots = []
         for k in range(GROUP):
             dz, dy, dc = offset(group, k)
-            spots.append(mod(z + dz, 4) * 8 + mod(y + dy, 4) * 2 + cs[dc])
+            spots.append(mod(z + 4 + hand * dz, 4) * 8 + mod(y + 4 + hand * dy, 4) * 2 + cs[dc])
         return spots
 
-    def sources(group):
+    def sources(group, hand=1):
         spots = []
         for k in range(GROUP):
             dz, dy, dc = offset(group, k)
-            spots.append(mod(z + 4 - dz, 4) * 8 + mod(y + 4 - dy, 4) * 2 + cs[dc])
+            spots.append(mod(z + 4 - hand * dz, 4) * 8 + mod(y + 4 - hand * dy, 4) * 2 + cs[dc])
         return spots
 
     def ends(chunk):
@@ -153,7 +152,7 @@
 
     def dispatch(chunk, group, count=GROUP):
         source, landing, sent, got = ends(chunk)
-        where = targets(group)
+        where = targets(group, 1 - 2 * chunk[0])
         for k in range(*count) if isinstance(count, tuple) else range(count):
             slot = GROUP * group + k
             pltpu.make_async_remote_copy(
@@ -166,14 +165,12 @@
             ).start()
 
     def dispatch_next(number):
-        @pl.when(number < 4 * GROUPS)
+        chunk, group = (0, lax.div(number, GROUPS)), lax.rem(number, GROUPS)
+        dispatch(chunk, group, GROUP - 1)
+
+        @pl.when(group < GROUPS - 1)
         def _():
-            chunk, group = (0, lax.div(number, GROUPS)), lax.rem(number, GROUPS)
-            dispatch(chunk, group, GROUP - 1)
-
-            @pl.when(group < GROUPS - 1)
-            def _():
-                dispatch(chunk, group, (GROUP - 1, GROUP))
+            dispatch(chunk, group, (GROUP - 1, GROUP))
 
     def arrive(chunk, group, count=GROUP):
         source, landing, _, got = ends(chunk)
@@ -195,8 +192,8 @@
             weights[f, i, 256:512, :] = swapped.astype(jnp.bfloat16)
     copies[1].wait()
 
-    def multiply(group, tile, weight):
-        where = targets(group)
+    def multiply(stage, group, tile, weight):
+        where = targets(group, 1 - 2 * stage)
         for i in range(2):
             for f in range(2):
                 tiles = [tile(f, i, d) for d in where]
@@ -206,7 +203,7 @@
                 prod[i, f] = jnp.dot(lhs, weight(f, i), preferred_element_type=jnp.float32)
 
     def emit(stage, jj, group, rank):
-        where = targets(group)
+        where = targets(group, 1 - 2 * stage)
         low = lax.broadcasted_iota(jnp.int32, (8, WIDTH), 1) < WIDTH // 2
         for k in range(GROUP):
             slot = GROUP * group + k
@@ -222,28 +219,29 @@
             send_a[2 * jj + 1, slot] = jnp.concatenate(right, axis=0).astype(jnp.bfloat16)
 
     def coefficients(stage, jj, tile, weight, rank, before=None, chunk=None):
-        multiply(0, tile, weight)
+        multiply(stage, 0, tile, weight)
         emit(stage, jj, 0, rank)
         if before is not None:
             before(1)
+        if chunk is not None:
             dispatch(chunk, 0)
-        multiply(1, tile, weight)
+        multiply(stage, 1, tile, weight)
+
+        if before is not None:
+            before(2)
+        emit(stage, jj, 1, rank)
+        multiply(stage, 2, tile, weight)
+        if before is not None:
+            before(3)
 
         def step(group, carry):
             if chunk is not None:
                 dispatch(chunk, group - 2)
             emit(stage, jj, group - 1, rank)
-            multiply(group, tile, weight)
+            multiply(stage, group, tile, weight)
             return carry
 
-        first = 2
-        if before is not None:
-            before(2)
-            emit(stage, jj, 1, rank)
-            multiply(2, tile, weight)
-            before(3)
-            first = 3
-        lax.fori_loop(first, GROUPS, step, 0)
+        lax.fori_loop(3, GROUPS, step, 0)
         if chunk is not None:
             dispatch(chunk, GROUPS - 2)
         emit(stage, jj, GROUPS - 1, rank)
@@ -283,8 +281,8 @@
     with scope("adj0"):
         u_copy(1).wait()
         adjoint(0, before=loaded, chunk=(0, 0))
-        for group in range(LEAD):
-            dispatch((0, 1), group)
+        for group in range(GROUPS):
+            dispatch((0, 1), group, GROUP - (group == GROUPS - 1))
     with scope("adj1"):
         adjoint(1)
 
@@ -335,7 +333,7 @@
 
     def take_back(chunk, group, last=False):
         jj = chunk[1]
-        whence = sources(group)
+        whence = sources(group, -1)
         stacks = [[[], []], [[], []]]
         for k in range(GROUP):
             slot = slot_of(group, k, last)
@@ -350,7 +348,7 @@
 
     def add_back(chunk, group):
         jj = chunk[1]
-        whence = sources(group)
+        whence = sources(group, -1)
         for f in range(2):
             for i in range(2):
                 held = turns[f, i]
@@ -360,31 +358,40 @@
                     total = total + jnp.dot(lhs, rhs, preferred_element_type=jnp.float32)
                 r_acc[f, i] = total
 
-    def gather(chunk, ahead=False):
+    def gather(chunk, first=0, stop=GROUPS, follow=None):
         unpack_group, add_group = ((take, add), (take_back, add_back))[chunk[0]]
-        arrive(chunk, 0)
-        first = (chunk[1] + 1) * GROUPS + LEAD
-        if ahead:
-            dispatch_next(first + zero)
-        unpack_group(chunk, 0)
+        if first == 0:
+            arrive(chunk, 0)
+            if follow is not None:
+                follow(zero)
+            unpack_group(chunk, 0)
+            first = 1
 
         def step(group, carry):
             arrive(chunk, group)
-            if ahead:
-                dispatch_next(first + group)
+            if follow is not None:
+                follow(group)
             add_group(chunk, group - 1)
             unpack_group(chunk, group)
             return carry
 
-        lax.fori_loop(1, GROUPS - 1, step, 0)
-        arrive(chunk, GROUPS - 1, GROUP - 1)
-        if ahead:
-            dispatch_next(first + zero + GROUPS - 1)
-        add_group(chunk, GROUPS - 2)
-        unpack_group(chunk, GROUPS - 1, True)
-        add_group(chunk, GROUPS - 1)
+        lax.fori_loop(first, min(stop, GROUPS - 1), step, 0)
+        if stop == GROUPS:
+            arrive(chunk, GROUPS - 1, GROUP - 1)
+            if follow is not None:
+                follow(zero + GROUPS - 1)
+            add_group(chunk, GROUPS - 2)
+            unpack_group(chunk, GROUPS - 1, True)
+            add_group(chunk, GROUPS - 1)
 
     zero = mod(fx, 1)
+
+    def two_more(group):
+        dispatch_next(2 * GROUPS + 2 * group)
+        dispatch_next(2 * GROUPS + 2 * group + 1)
+
+    def one_more(first):
+        return lambda group: dispatch_next(first + group)
 
     def clear():
         z_acc[...] = jnp.zeros_like(z_acc)
@@ -438,13 +445,13 @@
     for dz in (1, 2, 3, 0):
         v_copy(dz).wait()
     with scope("gather00"):
-        gather((0, 0), True)
+        gather((0, 0), follow=one_more(2 * GROUPS))
         share(0, 0)
     with scope("gather01"):
-        gather((0, 1), True)
+        gather((0, 1), follow=one_more(3 * GROUPS))
         share(0, 1)
-    with scope("gather10"):
-        gather((0, 2), True)
+    with scope("gather10a"):
+        gather((0, 2), 0, 8)
         share(1, 0)
     with scope("mix0"):
         mix(0, 0)

time: 56.7 us -> 56.4 us (level)
  no operation moved by 1% of the time
where the time goes in v3:
time: 56.4 us; the launch traced here: 56.3 us
  Pallas kernels  55.6 us (99%)
  local copies, waits for them, and re-layouts  0.71 us (1%)
    pallas_call x1, Pallas kernels, local(): pl.pallas_call(kernel, out_shape=pltpu.VMEM(u_data.shape, bf16), in_specs...  55.6 us

profile of v3, /device:TPU:1, one launch (start us, length us, event | category | flops | bytes accessed | tf_op | source)
XLA Modules:
  0.0 56.3 jit_solution(726277550107213660)
XLA Ops:
  0.0 55.6 %fused.1 = bf16[2,512,128]{2,1,0:T(8,128)(2,1)S(1)} custom-call(bf16[2,512,128]{2,1,0:T(8,128)(2,1)} %u_hbm.1, bf16[2,2,64,2,48,256]{5,4,3,2,1,0:T(8,128)(2,1)} %ub_hbm.1, bf16[2,64,2,2,48,256]{5,4,3,2,1,0:T(8,128)(2,1)} %vb_hbm.1, s32[2,64,64]{2,1,0:T(8,128)} %ranks_hbm.1, s32[64,64]{1,0:T(8,128)} %mask_hbm.1, f32[64,128]{1,0:T(8,128)} %constant.2.clone.table_hbm), custom_call_target="tpu_custom_call" | custom-call | tf_op jit(solution)/shard_map/fused/pallas_call | solution.py:496
  55.6 0.7 %copy.8 = bf16[2,512,128]{2,1,0:T(8,128)(2,1)} copy(bf16[2,512,128]{2,1,0:T(8,128)(2,1)S(1)} %fused.1) | data formatting | bytes 524288
